TPU v7x, 32 devices: a whole 2x2x4 slice. The times are simulated.
32 devices in a mesh: pipe: 8 (over z, y), dp: 4 (over x, core).
Axes of the slice: x: 2, y: 2, z: 4, core: 2. Of those that a mesh axis runs over, the one named last changes fastest.
Arguments:
- grad_output: bfloat16 [512, 8192], P('dp'), may hold values from -6 to 6
- hidden: bfloat16 [512, 14336], P('dp', 'pipe'), may hold values from -6 to 6
- next_hidden: bfloat16 [512, 14336], P('dp', 'pipe'), may hold values from -6 to 6
- master: float32 [14336, 8192], P('pipe', 'dp'), may hold values from -0.046875 to 0.046875
- moment: float32 [14336, 8192], P('pipe', 'dp'), may hold values from -24 to 24
- second_moment: float32 [14336, 8192], P('pipe', 'dp'), may hold values from 5 to 100
Outputs:
- update: float32 [14336, 8192], P('pipe', 'dp')
- upstream_grad: bfloat16 [512, 14336], P('dp', 'pipe')
- next_output: bfloat16 [512, 8192], P('pipe', 'dp')
All inputs are finite; a program needn't handle non-finite values.
Results may differ from a plain program's by a relative error of at most 0.005.
Values may be sent and summed in bfloat16 or wider, within the bound.
A program may use at most 256 MiB of HBM per device.

v0:
```python
import jax
import jax.numpy as jnp
from jax import lax
from jax.sharding import PartitionSpec as P

beta_one = 0.9
beta_two = 0.95
corr_one = 1.0 - 0.9**10
corr_two = 1.0 - 0.95**10
learn_rate = 0.005
decay_rate = 0.1
epsilon = 1e-08


def on_device(grad_output, hidden, next_hidden, master, moment, second_moment):
    weights_low = master.astype(jnp.bfloat16)
    columns = lax.all_to_all(grad_output, "dp", split_axis=1, concat_axis=0, tiled=True)
    rows_part = columns
    hidden_sum = lax.psum_scatter(
        lax.dot_general(
            rows_part, weights_low, (((1,), (1,)), ((), ())), preferred_element_type=jnp.float32
        ),
        "dp",
        scatter_dimension=0,
        tiled=True,
    )
    upstream = hidden_sum.astype(jnp.bfloat16)
    gathered = lax.all_gather(hidden, "dp", axis=0, tiled=True)
    gradient = lax.dot_general(
        gathered, columns, (((0,), (0,)), ((), ())), preferred_element_type=jnp.float32
    )
    moment_new = beta_one * moment + (1.0 - beta_one) * gradient
    second_new = beta_two * second_moment + (1.0 - beta_two) * gradient * gradient
    update = -(
        moment_new / corr_one / (jnp.sqrt(second_new / corr_two) + epsilon) + decay_rate * master
    )
    fresh_low = (master + learn_rate * update).astype(jnp.bfloat16)
    later_rows = lax.all_gather(next_hidden, "dp", axis=0, tiled=True)
    rows_part = later_rows
    next_out = lax.psum_scatter(
        jnp.dot(rows_part, fresh_low, preferred_element_type=jnp.float32),
        "pipe",
        scatter_dimension=0,
        tiled=True,
    ).astype(jnp.bfloat16)
    return (update, upstream, next_out)


def solution(mesh):
    in_specs = (
        P("dp", None),
        P("dp", "pipe"),
        P("dp", "pipe"),
        P("pipe", "dp"),
        P("pipe", "dp"),
        P("pipe", "dp"),
    )
    out_specs = (P("pipe", "dp"), P("dp", "pipe"), P("pipe", "dp"))
    return jax.shard_map(
        on_device, mesh=mesh, in_specs=in_specs, out_specs=out_specs, check_vma=False
    )
```

profile of v0, /device:TPU:0, one launch (start us, length us, event | category | flops | bytes accessed | tf_op | source)
XLA Modules:
  0.0 211.2 jit_solution(2200444903130895348)
XLA Ops:
  7.2 0.0 all-gather.3.cloned.1.call-start
  7.2 0.7 all-gather.3.cloned.1.call-update
  7.9 4.1 %copy.14 = bf16[128,8192]{0,1:T(8,128)(2,1)} copy(bf16[128,8192]{1,0:T(8,128)(2,1)} %param.6) | data formatting | bytes 4194304 | tf_op args[0]
  12.0 4.2 %all-to-all-start = ((bf16[128,4,2048]{0,2,1:T(8,128)(2,1)}), bf16[128,4,2048]{0,2,1:T(8,128)(2,1)S(1)}, u32[]{:S(2)}, u32[]{:S(2)}) async-start(bf16[128,4,2048]{0,2,1:T(8,128)(2,1)} %bitcast.11), calls=%async_computation | async-start | bytes 4194304 | tf_op jit(solution)/shard_map/all_to_all | solution.py:17
  16.2 0.0 all-gather.5.cloned.1.call-start
  16.2 0.7 all-gather.5.cloned.1.call-update
  16.9 0.0 reduce-scatter.5.cloned.1.call-start
  17.0 34.7 %all-to-all-done = bf16[128,4,2048]{0,2,1:T(8,128)(2,1)S(1)} async-done(((bf16[128,4,2048]{0,2,1:T(8,128)(2,1)}), bf16[128,4,2048]{0,2,1:T(8,128)(2,1)S(1)}, u32[]{:S(2)}, u32[]{:S(2)}) %all-to-all-start) | async-done | bytes 2097184 | tf_op jit(solution)/shard_map/all_to_all | solution.py:17
  51.7 2.6 %copy.15 = bf16[4,128,2048]{2,1,0:T(8,128)(2,1)} copy(bf16[4,128,2048]{1,2,0:T(8,128)(2,1)S(1)} %bitcast.10) | data formatting | bytes 4194304 | tf_op jit(solution)/shard_map/all_to_all | solution.py:17
  54.3 0.0 copy-start
  54.3 11.8 %fusion.9 = f32[512,1792]{1,0:T(8,128)} fusion(bf16[512,2048]{1,0:T(8,128)(2,1)} %bitcast.12, f32[1792,2048]{1,0:T(8,128)} %param.9), kind=kOutput, calls=%fused_computation.11 | convolution fusion | flops 3761766400 | bytes 20447232 | tf_op jit(solution)/shard_map/dot_general | solution.py:20
  66.1 0.0 reduce-scatter.5.cloned.1.call-update
  66.1 0.2 reduce-scatter.7.cloned.1.call-start
  66.4 0.0 all-gather.3.cloned.1.call-done
  66.4 0.0 copy-done
  66.4 25.2 %fusion.6 = f32[1792,2048]{1,0:T(8,128)} fusion(f32[1792,2048]{1,0:T(8,128)} %param.9, f32[1792,2048]{1,0:T(8,128)} %param.11, f32[1792,2048]{1,0:T(8,128)} %param.10, bf16[512,1792]{1,0:T(8,128)(2,1)} %all-gather.3.cloned.1.call-done, bf16[512,2048]{1,0:T(8,128)(2,1)S(1)} %bitcast.13), kind=kOutput, calls=%fused_computation.8 | convolution fusion | flops 3809476608 | bytes 62652416 | tf_op jit(solution)/shard_map/dot_general | solution.py:29
  91.6 0.0 all-gather.5.cloned.1.call-done
  91.6 16.1 %fusion.11 = f32[512,2048]{0,1:T(8,128)} fusion(bf16[512,1792]{1,0:T(8,128)(2,1)} %all-gather.5.cloned.1.call-done, f32[1792,2048]{1,0:T(8,128)} %param.9, f32[1792,2048]{1,0:T(8,128)} %fusion.6), kind=kOutput, calls=%fused_computation.13 | convolution fusion | flops 3769106432 | bytes 35389440 | tf_op jit(solution)/shard_map/dot_general | solution.py:41
  107.8 5.5 %copy.17 = f32[512,2048]{1,0:T(8,128)} copy(f32[512,2048]{0,1:T(8,128)} %fusion.11) | data formatting | bytes 8388608
  113.2 0.0 reduce-scatter.7.cloned.1.call-update
  113.2 0.0 reduce-scatter.5.cloned.1.call-done
  113.3 2.0 convert_element_type.13
  115.3 87.2 %reduce-scatter.7.cloned.1.call-done = f32[64,2048]{1,0:T(8,128)} async-done(((f32[512,2048]{1,0:T(8,128)}), f32[64,2048]{1,0:T(8,128)}) %reduce-scatter.7.cloned.1.call-update) | async-done | bytes 524304
  202.5 1.3 copy.18
  203.8 0.9 copy.16
Async XLA Ops:
  7.2 59.2 %all-gather.3.cloned.1.call-start = ((), (), s32[]{:S(2)}) async-start(), calls=%async_computation.3 | async-start | bytes 2293760 | tf_op jit(solution)/shard_map/all_gather | solution.py:28
  12.0 39.7 %all-to-all-start = ((bf16[128,4,2048]{0,2,1:T(8,128)(2,1)}), bf16[128,4,2048]{0,2,1:T(8,128)(2,1)S(1)}, u32[]{:S(2)}, u32[]{:S(2)}) async-start(bf16[128,4,2048]{0,2,1:T(8,128)(2,1)} %bitcast.11), calls=%async_computation | async-start | bytes 4194304 | tf_op jit(solution)/shard_map/all_to_all | solution.py:17
  16.2 75.4 %all-gather.5.cloned.1.call-start = ((), (), s32[]{:S(2)}) async-start(), calls=%async_computation.5 | async-start | bytes 2293760 | tf_op jit(solution)/shard_map/all_gather | solution.py:38
  16.9 96.4 %reduce-scatter.5.cloned.1.call-start = ((), (), s32[]{:S(2)}) async-start(), calls=%async_computation.4 | async-start | bytes 4587520 | tf_op jit(solution)/shard_map/reduce_scatter | solution.py:19
  54.3 12.1 %copy-start = (bf16[4,128,2048]{2,1,0:T(8,128)(2,1)S(1)}, bf16[4,128,2048]{2,1,0:T(8,128)(2,1)}, u32[]{:S(2)}) copy-start(bf16[4,128,2048]{2,1,0:T(8,128)(2,1)} %copy.15) | copy-start | bytes 6291460
  66.1 136.3 %reduce-scatter.7.cloned.1.call-start = ((), (), s32[]{:S(2)}) async-start(), calls=%async_computation.6 | async-start | bytes 4718592
Sparse Core Ops, SparseCore 0:
  9.6 33.7 all-gather.2
  44.9 21.0 all-gather.4
  68.6 41.2 reduce-scatter.4
  113.8 88.6 reduce-scatter.6
where the time goes:
time: 212 us; the launch traced here: 211 us
  waiting for transfers between devices  123 us (58%)
  matrix products  53.2 us (25%)
  local copies, waits for them, and re-layouts  14.3 us (7%)
  between operations  13.8 us (7%)
  starting transfers between devices  4.51 us (2%)
    unnamed x5, waiting for transfers between devices  88.6 us
    all_to_all x1, waiting for transfers between devices, on_device(): lax.all_to_all(grad_output, 'dp', split_axis=1, concat_axis=0, tiled=True)  34.7 us
    dot_general x1, matrix products, on_device(): lax.dot_general(gathered, columns, (((0,), (0,)), ((), ())), preferred_el...  25.2 us
    dot_general x1, matrix products, on_device(): jnp.dot(rows_part, fresh_low, preferred_element_type=jnp.float32)  16.1 us
    dot_general x1, matrix products, on_device(): lax.dot_general(rows_part, weights_low, (((1,), (1,)), ((), ())), preferr...  11.8 us
    unnamed x6, local copies, waits for them, and re-layouts  11.8 us
  transfers between devices with their start and end apart: 5, of which 2 were waited for; matrix products, arithmetic and copies ran while one was open for 32% of the time, Pallas kernels for 0%

commit v1 on v0

--- a/solution.py
+++ b/solution.py
@@ -14,7 +14,20 @@
 
 def on_device(grad_output, hidden, next_hidden, master, moment, second_moment):
     weights_low = master.astype(jnp.bfloat16)
-    columns = lax.all_to_all(grad_output, "dp", split_axis=1, concat_axis=0, tiled=True)
+    later, d_next = (lax.psum(1, "dp"), lax.axis_index("dp"))
+    current_value = grad_output.shape[1] // later
+    left_arr = list(grad_output.shape)
+    left_arr[1] = current_value
+    z2 = left_arr[0]
+    left_arr[0] = z2 * later
+    columns = jnp.zeros(left_arr, grad_output.dtype)
+    for t in range(later):
+        block_out = lax.dynamic_slice_in_dim(
+            grad_output, (d_next ^ t) * current_value, current_value, axis=1
+        )
+        if t:
+            block_out = lax.ppermute(block_out, "dp", [(q, q ^ t) for q in range(later)])
+        columns = lax.dynamic_update_slice_in_dim(columns, block_out, (d_next ^ t) * z2, axis=0)
     rows_part = columns
     hidden_sum = lax.psum_scatter(
         lax.dot_general(

time: 212 us -> 247 us (1.17)
  local copies, waits for them, and re-layouts: 14.3 us -> 70.2 us
  waiting for transfers between devices: 123 us -> 106 us
  matrix products: 53.2 us -> 50.7 us
    unnamed x6 -> x7, local copies, waits for them, and re-layouts: 11.8 us -> 66 us
    all_to_all x1 -> x0, waiting for transfers between devices: 34.7 us -> none  [on_device(): lax.all_to_all(grad_output, 'dp', split_axis=1, concat_axis=0, tiled=True)]
    ppermute x0 -> x3, waiting for transfers between devices: none -> 32.4 us  [on_device(): lax.ppermute(block_out, 'dp', [(q, q ^ t) for q in range(later)])]
    unnamed x5, waiting for transfers between devices: 88.6 us -> 73.8 us
    all_to_all x1 -> x0, starting transfers between devices: 4.21 us -> none  [on_device(): lax.all_to_all(grad_output, 'dp', split_axis=1, concat_axis=0, tiled=True)]
    ppermute x0 -> x3, starting transfers between devices: none -> 3.09 us  [on_device(): lax.ppermute(block_out, 'dp', [(q, q ^ t) for q in range(later)])]
    dynamic_slice x0 -> x1, local copies, waits for them, and re-layouts: none -> 2.75 us  [on_device(): lax.dynamic_slice_in_dim(grad_output, (d_next ^ t) * current_value, curre...]
    all_to_all x1 -> x0, local copies, waits for them, and re-layouts: 2.58 us -> none  [on_device(): lax.all_to_all(grad_output, 'dp', split_axis=1, concat_axis=0, tiled=True)]
  transfers between devices with their start and end apart: 5 -> 7, of which waited for: 2 -> 3; matrix products, arithmetic and copies ran while one was open for 32% -> 49% of each run, Pallas kernels for 0% -> 0%
where the time goes in v1:
time: 247 us; the launch traced here: 246 us
  waiting for transfers between devices  106 us (43%)
  local copies, waits for them, and re-layouts  70.2 us (28%)
  matrix products  50.7 us (21%)
  between operations  13.8 us (6%)
  starting transfers between devices  3.42 us (1%)
    unnamed x5, waiting for transfers between devices  73.8 us
    unnamed x7, local copies, waits for them, and re-layouts  66 us
    ppermute x3, waiting for transfers between devices, on_device(): lax.ppermute(block_out, 'dp', [(q, q ^ t) for q in range(later)])  32.4 us
    dot_general x1, matrix products, on_device(): lax.dot_general(gathered, columns, (((0,), (0,)), ((), ())), preferred_el...  25.2 us
    dot_general x1, matrix products, on_device(): jnp.dot(rows_part, fresh_low, preferred_element_type=jnp.float32)  15.8 us
    dot_general x1, matrix products, on_device(): lax.dot_general(rows_part, weights_low, (((1,), (1,)), ((), ())), preferr...  9.69 us
  transfers between devices with their start and end apart: 7, of which 3 were waited for; matrix products, arithmetic and copies ran while one was open for 49% of the time, Pallas kernels for 0%

profile of v1, /device:TPU:0, one launch (start us, length us, event | category | flops | bytes accessed | tf_op | source)
XLA Modules:
  0.0 246.3 jit_solution(3590247845730653552)
XLA Ops:
  7.2 0.0 all-gather.3.cloned.1.call-start
  7.2 0.7 all-gather.3.cloned.1.call-update
  7.9 0.0 all-gather.5.cloned.1.call-start
  7.9 0.7 all-gather.5.cloned.1.call-update
  8.6 0.0 reduce-scatter.5.cloned.1.call-start
  8.7 0.2 broadcast_in_dim.3
  9.0 2.7 %constant_dynamic-slice_fusion = (bf16[128,2048]{1,0:T(8,128)(2,1)}, bf16[128,2048]{1,0:T(8,128)(2,1)}, bf16[512,2048]{1,0:T(8,128)(2,1)S(1)}, bf16[128,2048]{1,0:T(8,128)(2,1)}) fusion(bf16[128,8192]{1,0:T(8,128)(2,1)} %param.6, s32[]{:T(128)S(6)} %select_n.30, s32[]{:T(128)S(6)} %select_n.26, bf16[512,2048]{1,0:T(8,128)(2,1)S(1)} %broadcast_in_dim.3, ...), kind=kLoop, calls=%fused_computation.18 | loop fusion | bytes 4194324 | tf_op jit(solution)/shard_map/dynamic_slice | solution.py:25
  11.7 0.5 collective-permute-start
  12.2 2.5 %collective-permute-start.1 = (bf16[128,2048]{1,0:T(8,128)(2,1)}, bf16[128,2048]{1,0:T(8,128)(2,1)S(1)}, u32[]{:S(2)}, u32[]{:S(2)}) collective-permute-start(bf16[128,2048]{1,0:T(8,128)(2,1)} %get-tuple-element.12), channel_id=1, source_target_pairs={{0,2},{1,3},{2,0},{3,1},{4,6},{5,7},{6,4},{7,5},{8,10},{9,11},{10,... | collective-permute-start | bytes 1572872 | tf_op jit(solution)/shard_map/ppermute | solution.py:29
  14.7 0.1 collective-permute-start.2
  14.8 0.0 collective-permute-done
  14.8 1.1 constant_dynamic-update-slice_fusion.1
  15.9 18.4 %collective-permute-done.1 = bf16[128,2048]{1,0:T(8,128)(2,1)S(1)} collective-permute-done((bf16[128,2048]{1,0:T(8,128)(2,1)}, bf16[128,2048]{1,0:T(8,128)(2,1)S(1)}, u32[]{:S(2)}, u32[]{:S(2)}) %collective-permute-start.1) | collective-permute-done | bytes 524320 | tf_op jit(solution)/shard_map/ppermute | solution.py:29
  34.3 14.0 %collective-permute-done.2 = bf16[128,2048]{1,0:T(8,128)(2,1)S(1)} collective-permute-done((bf16[128,2048]{1,0:T(8,128)(2,1)}, bf16[128,2048]{1,0:T(8,128)(2,1)S(1)}, u32[]{:S(2)}, u32[]{:S(2)}) %collective-permute-start.2) | collective-permute-done | bytes 524320 | tf_op jit(solution)/shard_map/ppermute | solution.py:29
  48.4 9.7 %fusion.11 = f32[512,1792]{1,0:T(8,128)} fusion(bf16[512,2048]{1,0:T(8,128)(2,1)S(1)} %constant_dynamic-update-slice_fusion.2, f32[1792,2048]{1,0:T(8,128)} %param.9), kind=kOutput, calls=%fused_computation.14 | convolution fusion | flops 3761766400 | bytes 20447232 | tf_op jit(solution)/shard_map/dot_general | solution.py:33
  58.1 0.0 reduce-scatter.5.cloned.1.call-update
  58.1 0.2 reduce-scatter.7.cloned.1.call-start
  58.3 14.3 %copy.17 = f32[1792,2048]{0,1:T(8,128)} copy(f32[1792,2048]{1,0:T(8,128)} %param.9) | data formatting | bytes 29360128 | tf_op args[3]
  72.6 14.5 %copy.15 = f32[1792,2048]{0,1:T(8,128)} copy(f32[1792,2048]{1,0:T(8,128)} %param.10) | data formatting | bytes 29360128 | tf_op args[4]
  87.1 14.4 %copy.16 = f32[1792,2048]{0,1:T(8,128)} copy(f32[1792,2048]{1,0:T(8,128)} %param.11) | data formatting | bytes 29360128 | tf_op args[5]
  101.5 0.0 all-gather.3.cloned.1.call-done
  101.5 25.2 %fusion.8 = f32[1792,2048]{0,1:T(8,128)} fusion(f32[1792,2048]{0,1:T(8,128)} %copy.17, f32[1792,2048]{0,1:T(8,128)} %copy.16, f32[1792,2048]{0,1:T(8,128)} %copy.15, bf16[512,2048]{1,0:T(8,128)(2,1)S(1)} %constant_dynamic-update-slice_fusion.2, bf16[512,1792]{1,0:T(8,128)(2,1)} %all-gather.3.cloned.1.call-done), kind=kOutput, calls=%fused_computation.11 | convolution fusion | flops 3809476608 | bytes 62652416 | tf_op jit(solution)/shard_map/dot_general | solution.py:42
  126.7 0.0 all-gather.5.cloned.1.call-done
  126.7 15.8 %fusion.13 = f32[512,2048]{0,1:T(8,128)} fusion(bf16[512,1792]{1,0:T(8,128)(2,1)} %all-gather.5.cloned.1.call-done, f32[1792,2048]{0,1:T(8,128)} %copy.17, f32[1792,2048]{0,1:T(8,128)} %fusion.8), kind=kOutput, calls=%fused_computation.16 | convolution fusion | flops 3769106432 | bytes 35389440 | tf_op jit(solution)/shard_map/dot_general | solution.py:54
  142.5 5.4 %copy.21 = f32[512,2048]{1,0:T(8,128)} copy(f32[512,2048]{0,1:T(8,128)} %fusion.13) | data formatting | bytes 8388608
  147.9 0.0 reduce-scatter.7.cloned.1.call-update
  147.9 15.2 %copy.19 = f32[1792,2048]{1,0:T(8,128)} copy(f32[1792,2048]{0,1:T(8,128)} %fusion.8) | data formatting | bytes 29360128
  163.2 0.0 reduce-scatter.5.cloned.1.call-done
  163.2 2.0 convert_element_type.13
  165.2 72.4 %reduce-scatter.7.cloned.1.call-done = f32[64,2048]{1,0:T(8,128)} async-done(((f32[512,2048]{1,0:T(8,128)}), f32[64,2048]{1,0:T(8,128)}) %reduce-scatter.7.cloned.1.call-update) | async-done | bytes 524304
  237.6 1.3 copy.22
  238.9 0.9 copy.20
  (2 shorter events, 0.1 us)
Async XLA Ops:
  7.2 94.4 %all-gather.3.cloned.1.call-start = ((), (), s32[]{:S(2)}) async-start(), calls=%async_computation.2 | async-start | bytes 2293760 | tf_op jit(solution)/shard_map/all_gather | solution.py:41
  7.9 118.8 %all-gather.5.cloned.1.call-start = ((), (), s32[]{:S(2)}) async-start(), calls=%async_computation.4 | async-start | bytes 2293760 | tf_op jit(solution)/shard_map/all_gather | solution.py:51
  8.6 154.5 %reduce-scatter.5.cloned.1.call-start = ((), (), s32[]{:S(2)}) async-start(), calls=%async_computation.3 | async-start | bytes 4587520 | tf_op jit(solution)/shard_map/reduce_scatter | solution.py:32
  11.7 3.1 %collective-permute-start = (bf16[128,2048]{1,0:T(8,128)(2,1)}, bf16[128,2048]{1,0:T(8,128)(2,1)}, u32[]{:S(2)}, u32[]{:S(2)}) collective-permute-start(bf16[128,2048]{1,0:T(8,128)(2,1)} %get-tuple-element.10), channel_id=1, source_target_pairs={{0,1},{1,0},{2,3},{3,2},{4,5},{5,4},{6,7},{7,6},{8,9},{9,8},{10,11... | collective-permute-start | bytes 1572872 | tf_op jit(solution)/shard_map/ppermute | solution.py:29
  12.2 22.1 %collective-permute-start.1 = (bf16[128,2048]{1,0:T(8,128)(2,1)}, bf16[128,2048]{1,0:T(8,128)(2,1)S(1)}, u32[]{:S(2)}, u32[]{:S(2)}) collective-permute-start(bf16[128,2048]{1,0:T(8,128)(2,1)} %get-tuple-element.12), channel_id=1, source_target_pairs={{0,2},{1,3},{2,0},{3,1},{4,6},{5,7},{6,4},{7,5},{8,10},{9,11},{10,... | collective-permute-start | bytes 1572872 | tf_op jit(solution)/shard_map/ppermute | solution.py:29
  14.7 33.7 %collective-permute-start.2 = (bf16[128,2048]{1,0:T(8,128)(2,1)}, bf16[128,2048]{1,0:T(8,128)(2,1)S(1)}, u32[]{:S(2)}, u32[]{:S(2)}) collective-permute-start(bf16[128,2048]{1,0:T(8,128)(2,1)} %get-tuple-element.9), channel_id=1, source_target_pairs={{0,3},{1,2},{2,1},{3,0},{4,7},{5,6},{6,5},{7,4},{8,11},{9,10},{10,... | collective-permute-start | bytes 1572872 | tf_op jit(solution)/shard_map/ppermute | solution.py:29
  58.1 179.5 %reduce-scatter.7.cloned.1.call-start = ((), (), s32[]{:S(2)}) async-start(), calls=%async_computation.5 | async-start | bytes 4718592
Sparse Core Ops, SparseCore 0:
  9.6 33.7 all-gather.2
  44.9 21.1 all-gather.4
  68.6 41.2 reduce-scatter.4
  148.1 89.4 reduce-scatter.6
